TPU v7x, 32 devices: a whole 2x2x4 slice. The times are simulated.
32 devices in a mesh: dp: 4 (over z), seq: 8 (over y, x, core).
Axes of the slice: x: 2, y: 2, z: 4, core: 2. Of those that a mesh axis runs over, the one named last changes fastest.
Arguments:
- frames_in: bfloat16 [4, 4096, 1024], P('dp', 'seq'), may hold values from -16 to 16
- memory_in: bfloat16 [4, 32, 1024], P('dp', 'seq'), may hold values from -6 to 6
- w_query: bfloat16 [1024, 1024], P(None, 'dp'), may hold values from -1 to 1
- w_key: bfloat16 [1024, 1024], P(None, 'dp'), may hold values from -1 to 1
- w_value: bfloat16 [1024, 1024], P(None, 'dp'), may hold values from -0.1875 to 0.1875
- lengths: int32 [4], P('dp'), may hold values from 1024 to 4096, as said below
Outputs:
- context: bfloat16 [4, 4096, 1024], P('dp', 'seq')
- memory_out: bfloat16 [4, 32, 1024], P('dp', 'seq')
Inputs may be any that keep to these rules, and one draw needn't show every extreme that they name: `lengths`: some utterance has all 4096 frames live; every utterance has at least a quarter of them.
All inputs are finite; a program needn't handle non-finite values.
Results may differ from a plain program's by a relative error of at most 0.0071.
Values may be sent and summed in bfloat16 or wider, within the bound.
No kernel may reach another device: no remote copies, remote signals or barrier semaphores. Data moves between devices by JAX's collectives and lax.ppermute only.
A program may use at most 64 MiB of HBM per device.

v0:
```python
import jax
import jax.numpy as jnp
from jax import lax
from jax.sharding import PartitionSpec as P

HEADS = 16
LEFT = 128
RIGHT = 32


def passed_along(block, axis, distance):
    devices = range(lax.axis_size(axis))
    route = [(i - distance, i) for i in devices if i - distance in devices]
    return lax.ppermute(block, axis, route)


def attend(queries, keys, values, key_live, scale):
    utt_count, n_query, feat_width = queries.shape
    n_key = keys.shape[1]
    q_heads = queries.reshape(utt_count, n_query, HEADS, -1)
    k_heads = keys.reshape(utt_count, n_key, HEADS, -1)
    v_heads = values.reshape(utt_count, n_key, HEADS, -1)
    scores = (
        jnp.einsum("bqhe,bkhe->bhqk", q_heads, k_heads, preferred_element_type=jnp.float32) * scale
    )
    scores = jnp.where(key_live[:, None, None, :], scores, -1e30)
    row_max = jnp.max(scores, axis=-1, keepdims=True)
    probs = jnp.exp(scores - row_max)
    weights = (probs / jnp.sum(probs, axis=-1, keepdims=True)).astype(jnp.bfloat16)
    mixed = jnp.einsum("bhqk,bkhe->bqhe", weights, v_heads, preferred_element_type=jnp.float32)
    return mixed.reshape(utt_count, n_query, feat_width)


def local(frames_in, memory_in, w_query, w_key, w_value, lengths):
    utt_count, row_count, feat_width = frames_in.shape
    seg_dev = memory_in.shape[1]
    seg_len = row_count // seg_dev
    key_span = LEFT + seg_len + RIGHT
    scale = float(feat_width // HEADS) ** (-0.5)
    seq_index = lax.axis_index("seq")
    row_base = seq_index * row_count
    frame_start = 0
    bank_rows = lax.all_gather(memory_in, "seq", axis=1, tiled=True)
    row_pos = row_base + jnp.arange(row_count, dtype=jnp.int32)
    live_mask = row_pos[None, :] < lengths[:, None]
    live_blocks = live_mask.reshape(utt_count, seg_dev, seg_len)
    masked_sums = jnp.einsum(
        "bnsd,bns->bnd",
        frames_in.reshape(utt_count, seg_dev, seg_len, feat_width),
        live_blocks.astype(jnp.bfloat16),
        preferred_element_type=jnp.float32,
    )
    counts = jnp.sum(live_blocks.astype(jnp.float32), axis=2)
    summary = (masked_sums / jnp.maximum(counts, 1.0)[:, :, None]).astype(jnp.bfloat16)
    n_frame = frames_in.shape[1]
    all_rows = jnp.concatenate([frames_in, summary, bank_rows], axis=1)
    n_total = all_rows.shape[1]
    flat_rows = all_rows.reshape(utt_count * n_total, feat_width)

    def project_one(piece):
        return jnp.dot(flat_rows, piece, preferred_element_type=jnp.float32).astype(jnp.bfloat16)

    q_flat = project_one(lax.all_gather(w_query, "dp", axis=1, tiled=True))
    k_flat = project_one(lax.all_gather(w_key, "dp", axis=1, tiled=True))
    v_flat = project_one(lax.all_gather(w_value, "dp", axis=1, tiled=True))
    q_all = q_flat.reshape(utt_count, n_total, feat_width)
    k_all = k_flat.reshape(utt_count, n_total, feat_width)
    v_all = v_flat.reshape(utt_count, n_total, feat_width)
    q_frames = q_all[:, frame_start : frame_start + row_count]
    q_summary = q_all[:, n_frame : n_frame + seg_dev]
    bank_keys = k_all[:, n_frame + seg_dev :]
    bank_values = v_all[:, n_frame + seg_dev :]
    k_own = k_all[:, :row_count]
    v_own = v_all[:, :row_count]
    k_before, v_before = passed_along(
        (k_own[:, row_count - LEFT :], v_own[:, row_count - LEFT :]), "seq", 1
    )
    k_after, v_after = passed_along((k_own[:, :RIGHT], v_own[:, :RIGHT]), "seq", -1)
    k_ext = jnp.concatenate([k_before, k_own, k_after], axis=1)
    v_ext = jnp.concatenate([v_before, v_own, v_after], axis=1)
    bank_count = bank_keys.shape[1]
    bank_index = jnp.arange(bank_count, dtype=jnp.int32)
    bank_ready = bank_index[None, :] * seg_len < lengths[:, None]

    def one_segment(seg_index):
        global_seg = seq_index * seg_dev + seg_index
        q_rows = lax.dynamic_slice_in_dim(q_frames, seg_index * seg_len, seg_len, 1)
        q_sum = lax.dynamic_slice_in_dim(q_summary, seg_index, 1, 1)
        queries = jnp.concatenate([q_rows, q_sum], axis=1)
        k_window = lax.dynamic_slice_in_dim(k_ext, seg_index * seg_len, key_span, 1)
        v_window = lax.dynamic_slice_in_dim(v_ext, seg_index * seg_len, key_span, 1)
        frame_pos = row_base - LEFT + seg_index * seg_len + jnp.arange(key_span, dtype=jnp.int32)
        frame_live = (frame_pos[None, :] >= 0) & (frame_pos[None, :] < lengths[:, None])
        key_live = jnp.concatenate(
            [bank_ready & (bank_index < global_seg)[None, :], frame_live], axis=1
        )
        keys = jnp.concatenate([bank_keys, k_window], axis=1)
        values = jnp.concatenate([bank_values, v_window], axis=1)
        return attend(queries, keys, values, key_live, scale)

    attended = lax.map(one_segment, jnp.arange(seg_dev, dtype=jnp.int32))
    frame_part = (
        attended[:, :, :seg_len].transpose(1, 0, 2, 3).reshape(utt_count, row_count, feat_width)
    )
    context = (frame_part * live_mask[:, :, None].astype(jnp.float32)).astype(jnp.bfloat16)
    memory_out = attended[:, :, seg_len].transpose(1, 0, 2).astype(jnp.bfloat16)
    return (context, memory_out)


def solution(mesh):
    placed = (
        P("dp", "seq", None),
        P("dp", "seq", None),
        P(None, "dp"),
        P(None, "dp"),
        P(None, "dp"),
        P("dp"),
    )
    return jax.shard_map(
        local,
        mesh=mesh,
        in_specs=placed,
        out_specs=(P("dp", "seq", None), P("dp", "seq", None)),
        check_vma=False,
    )
```

profile of v0, /device:TPU:3, one launch (start us, length us, event | category | flops | bytes accessed | tf_op | source)
XLA Modules:
  0.0 252.9 jit_solution(9510433819351743117)
XLA Ops:
  10.8 9.7 %all_gather.12 = bf16[1,32,1024]{2,0,1:T(2,128)(2,1)S(1)} all-gather(bf16[1,4,1024]{2,0,1:T(2,128)(2,1)S(1)} %copy.26), channel_id=1, replica_groups=mesh['dp'=4,'seq'=8] {'seq'}, dimensions={1}, use_global_device_ids=true | all-gather | bytes 73728 | tf_op jit(solution)/shard_map/all_gather | solution.py:43
  20.7 1.5 fusion.21
  22.3 34.8 %all-gather.4.cloned.1.call-done = bf16[1024,1024]{1,0:T(8,128)(2,1)} async-done(((bf16[1024,256]{1,0:T(8,128)(2,1)}), bf16[1024,1024]{1,0:T(8,128)(2,1)}) %all-gather.4.cloned.1.call-update) | async-done | bytes 2097168 | tf_op jit(solution)/shard_map/all_gather | solution.py:65
  57.1 2.9 %fusion.15 = bf16[1,548,1024]{2,1,0:T(8,128)(2,1)S(1)} fusion(bf16[1024,1024]{1,0:T(8,128)(2,1)} %all-gather.4.cloned.1.call-done, bf16[1,32,1024]{2,1,0:T(8,128)(2,1)S(1)} %copy.27, bf16[1,4,1024]{2,1,0:T(4,128)(2,1)S(1)} %fusion.20, bf16[1,512,1024]{2,1,0:T(8,128)(2,1)S(1)} %copy-done.3), kind=kOutput, calls=%fused_computation.30 | convolution fusion | flops 1153167360 | bytes 4341760 | tf_op jit(solution)/shard_map/dot_general | solution.py:61
  61.4 2.5 collective-permute-start.1
  64.0 3.9 %collective-permute-start = (bf16[1,128,1024]{2,1,0:T(8,128)(2,1)}, bf16[1,128,1024]{2,1,0:T(8,128)(2,1)}, u32[]{:S(2)}, u32[]{:S(2)}) collective-permute-start(bf16[1,128,1024]{2,1,0:T(8,128)(2,1)} %slice.53), channel_id=1, source_target_pairs={{0,1},{1,2},{2,3},{3,4},{4,5},{5,6},{6,7},{8,9},{9,10},{10,11},{11... | collective-permute-start | bytes 786440 | tf_op jit(solution)/shard_map/ppermute | solution.py:14
  67.9 35.3 %all-gather.8.cloned.1.call-done = bf16[1024,1024]{1,0:T(8,128)(2,1)} async-done(((bf16[1024,256]{1,0:T(8,128)(2,1)}), bf16[1024,1024]{1,0:T(8,128)(2,1)}) %all-gather.8.cloned.1.call-update) | async-done | bytes 2097168 | tf_op jit(solution)/shard_map/all_gather | solution.py:64
  103.1 2.9 %fusion.17 = bf16[1,548,1024]{2,1,0:T(8,128)(2,1)S(1)} fusion(bf16[1024,1024]{1,0:T(8,128)(2,1)} %all-gather.8.cloned.1.call-done, bf16[1,32,1024]{2,1,0:T(8,128)(2,1)S(1)} %copy.27, bf16[1,4,1024]{2,1,0:T(4,128)(2,1)S(1)} %fusion.20, bf16[1,512,1024]{2,1,0:T(8,128)(2,1)S(1)} %copy-done.3), kind=kOutput, calls=%fused_computation.32 | convolution fusion | flops 1153167360 | bytes 4341760 | tf_op jit(solution)/shard_map/dot_general | solution.py:61
  106.1 0.8 slice.59
  106.9 3.6 %collective-permute-start.2 = (bf16[1,128,1024]{2,1,0:T(8,128)(2,1)}, bf16[1,128,1024]{2,1,0:T(8,128)(2,1)}, u32[]{:S(2)}, u32[]{:S(2)}) collective-permute-start(bf16[1,128,1024]{2,1,0:T(8,128)(2,1)} %slice.59), channel_id=1, source_target_pairs={{0,1},{1,2},{2,3},{3,4},{4,5},{5,6},{6,7},{8,9},{9,10},{10,11},{11... | collective-permute-start | bytes 786440 | tf_op jit(solution)/shard_map/ppermute | solution.py:14
  110.5 38.7 %all-gather.6.cloned.1.call-done = bf16[1024,1024]{1,0:T(8,128)(2,1)} async-done(((bf16[1024,256]{1,0:T(8,128)(2,1)}), bf16[1024,1024]{1,0:T(8,128)(2,1)}) %all-gather.6.cloned.1.call-update) | async-done | bytes 2097168 | tf_op jit(solution)/shard_map/all_gather | solution.py:63
  149.2 2.9 %fusion.16 = bf16[1,548,1024]{2,1,0:T(8,128)(2,1)S(1)} fusion(bf16[1024,1024]{1,0:T(8,128)(2,1)} %all-gather.6.cloned.1.call-done, bf16[1,32,1024]{2,1,0:T(8,128)(2,1)S(1)} %copy.27, bf16[1,4,1024]{2,1,0:T(4,128)(2,1)S(1)} %fusion.20, bf16[1,512,1024]{2,1,0:T(8,128)(2,1)S(1)} %copy-done.3), kind=kOutput, calls=%fused_computation.31 | convolution fusion | flops 1153167360 | bytes 4341760 | tf_op jit(solution)/shard_map/dot_general | solution.py:61
  152.1 1.0 slice.54
  153.2 1.0 slice.57
  154.2 2.7 %collective-permute-start.3 = (bf16[1,32,1024]{2,1,0:T(8,128)(2,1)S(1)}, bf16[1,32,1024]{2,1,0:T(8,128)(2,1)S(1)}, u32[]{:S(2)}, u32[]{:S(2)}) collective-permute-start(bf16[1,32,1024]{2,1,0:T(8,128)(2,1)S(1)} %get-tuple-element.266), channel_id=1, source_target_pairs={{1,0},{2,1},{3,2},{4,3},{5,4},{6,5},{7,6},{9,8},{10,9},{11,10},{12... | collective-permute-start | bytes 196616 | tf_op jit(solution)/shard_map/ppermute | solution.py:14
  157.1 0.8 copy.33
  157.9 1.4 pad_maximum_fusion.3
  159.3 1.5 collective-permute-done.3
  160.9 2.2 pad_maximum_fusion.4
  163.1 72.8 %while.13 = (s32[]{:T(128)}, f32[4,1,129,1024]{2,3,1,0:T(8,128)}, s32[4]{0:T(128)S(1)}, bf16[1,672,1024]{2,1,0:T(8,128)(2,1)S(1)}, bf16[1,32,1024]{1,2,0:T(8,128...) while((s32[]{:T(128)}, f32[4,1,129,1024]{2,3,1,0:T(8,128)}, ...), condition=%wide.region_4.5_spmd.clone, body=%wide.region_1.4_spmd.clone.sunk | while | flops 176197520 | bytes 28918032 | solution.py:101
  164.9 1.1 constant_dynamic-slice_fusion.9
  166.3 1.8 pad_maximum_fusion.7
  168.2 1.0 constant_dynamic-slice_fusion.11
  173.7 3.0 %fusion.45 = (f32[16,129]{1,0:T(8,128)S(1)}, f32[16,129,320]{2,1,0:T(8,128)}) fusion(pred[320]{0:T(512)(128)(4,1)S(1)} %add_reduce_fusion.2, bf16[129,16,64]{0,2,1:T(8,128)(2,1)S(1)} %bitcast.76, bf16[320,16,64]{0,2,1:T(8,128)(2,1)S(1)} %bitcast.75), kind=kOutput, calls=%fused_computation.50.clone.1 | convolution fusion | flops 87183680 | bytes 3570048 | tf_op jit(solution)/shard_map/while/body/eval_jaxpr/sub | solution.py:28
  176.7 2.9 %fusion.46 = f32[16,64,129]{2,1,0:T(8,128)S(1)} fusion(bf16[320,16,64]{0,2,1:T(8,128)(2,1)S(1)} %bitcast.74, f32[16,129,320]{2,1,0:T(8,128)} %get-tuple-element.354, f32[16,129]{1,0:T(8,128)S(1)} %get-tuple-element.355), kind=kOutput, calls=%fused_computation.9.clone.1 | convolution fusion | flops 85862400 | bytes 3833920 | tf_op jit(solution)/shard_map/while/body/eval_jaxpr/bhqk,bkhe->bqhe/dot_general | solution.py:30
  179.6 1.0 constant_dynamic-update-slice_fusion.2
  183.1 1.1 constant_dynamic-slice_fusion.9
  184.6 1.8 pad_maximum_fusion.7
  186.4 1.0 constant_dynamic-slice_fusion.11
  191.9 3.0 %fusion.45 = (f32[16,129]{1,0:T(8,128)S(1)}, f32[16,129,320]{2,1,0:T(8,128)}) fusion(pred[320]{0:T(512)(128)(4,1)S(1)} %add_reduce_fusion.2, bf16[129,16,64]{0,2,1:T(8,128)(2,1)S(1)} %bitcast.76, bf16[320,16,64]{0,2,1:T(8,128)(2,1)S(1)} %bitcast.75), kind=kOutput, calls=%fused_computation.50.clone.1 | convolution fusion | flops 87183680 | bytes 3570048 | tf_op jit(solution)/shard_map/while/body/eval_jaxpr/sub | solution.py:28
  194.9 2.9 %fusion.46 = f32[16,64,129]{2,1,0:T(8,128)S(1)} fusion(bf16[320,16,64]{0,2,1:T(8,128)(2,1)S(1)} %bitcast.74, f32[16,129,320]{2,1,0:T(8,128)} %get-tuple-element.354, f32[16,129]{1,0:T(8,128)S(1)} %get-tuple-element.355), kind=kOutput, calls=%fused_computation.9.clone.1 | convolution fusion | flops 85862400 | bytes 3833920 | tf_op jit(solution)/shard_map/while/body/eval_jaxpr/bhqk,bkhe->bqhe/dot_general | solution.py:30
  197.8 1.1 constant_dynamic-update-slice_fusion.2
  201.3 1.1 constant_dynamic-slice_fusion.9
  202.8 1.8 pad_maximum_fusion.7
  204.6 1.0 constant_dynamic-slice_fusion.11
  210.1 3.0 %fusion.45 = (f32[16,129]{1,0:T(8,128)S(1)}, f32[16,129,320]{2,1,0:T(8,128)}) fusion(pred[320]{0:T(512)(128)(4,1)S(1)} %add_reduce_fusion.2, bf16[129,16,64]{0,2,1:T(8,128)(2,1)S(1)} %bitcast.76, bf16[320,16,64]{0,2,1:T(8,128)(2,1)S(1)} %bitcast.75), kind=kOutput, calls=%fused_computation.50.clone.1 | convolution fusion | flops 87183680 | bytes 3570048 | tf_op jit(solution)/shard_map/while/body/eval_jaxpr/sub | solution.py:28
  213.1 2.9 %fusion.46 = f32[16,64,129]{2,1,0:T(8,128)S(1)} fusion(bf16[320,16,64]{0,2,1:T(8,128)(2,1)S(1)} %bitcast.74, f32[16,129,320]{2,1,0:T(8,128)} %get-tuple-element.354, f32[16,129]{1,0:T(8,128)S(1)} %get-tuple-element.355), kind=kOutput, calls=%fused_computation.9.clone.1 | convolution fusion | flops 85862400 | bytes 3833920 | tf_op jit(solution)/shard_map/while/body/eval_jaxpr/bhqk,bkhe->bqhe/dot_general | solution.py:30
  216.0 1.0 constant_dynamic-update-slice_fusion.2
  219.5 1.1 constant_dynamic-slice_fusion.9
  221.0 1.8 pad_maximum_fusion.7
  222.8 1.0 constant_dynamic-slice_fusion.11
  228.3 3.0 %fusion.45 = (f32[16,129]{1,0:T(8,128)S(1)}, f32[16,129,320]{2,1,0:T(8,128)}) fusion(pred[320]{0:T(512)(128)(4,1)S(1)} %add_reduce_fusion.2, bf16[129,16,64]{0,2,1:T(8,128)(2,1)S(1)} %bitcast.76, bf16[320,16,64]{0,2,1:T(8,128)(2,1)S(1)} %bitcast.75), kind=kOutput, calls=%fused_computation.50.clone.1 | convolution fusion | flops 87183680 | bytes 3570048 | tf_op jit(solution)/shard_map/while/body/eval_jaxpr/sub | solution.py:28
  231.3 2.9 %fusion.46 = f32[16,64,129]{2,1,0:T(8,128)S(1)} fusion(bf16[320,16,64]{0,2,1:T(8,128)(2,1)S(1)} %bitcast.74, f32[16,129,320]{2,1,0:T(8,128)} %get-tuple-element.354, f32[16,129]{1,0:T(8,128)S(1)} %get-tuple-element.355), kind=kOutput, calls=%fused_computation.9.clone.1 | convolution fusion | flops 85862400 | bytes 3833920 | tf_op jit(solution)/shard_map/while/body/eval_jaxpr/bhqk,bkhe->bqhe/dot_general | solution.py:30
  234.2 1.1 constant_dynamic-update-slice_fusion.2
  235.9 3.0 %slice.51 = f32[4,1,128,1024]{2,3,1,0:T(8,128)} slice(f32[4,1,129,1024]{2,3,1,0:T(8,128)} %get-tuple-element.165), slice={[0:4], [0:1], [0:128], [0:1024]} | slice | bytes 4194304 | tf_op jit(solution)/shard_map/slice | solution.py:103
  239.0 3.7 %copy.35 = bf16[4,1,129,1024]{3,0,2,1:T(4,128)(2,1)S(1)} copy(f32[4,1,129,1024]{2,3,1,0:T(8,128)} %get-tuple-element.165) | data formatting | bytes 3170304 | tf_op jit(solution)/shard_map/while | solution.py:101
  242.7 1.9 copy.34
  245.2 1.1 fusion.14
  (90 shorter events, 21.2 us)
Async XLA Ops:
  7.2 49.9 %copy-start.3 = (bf16[1,512,1024]{2,1,0:T(8,128)(2,1)S(1)}, bf16[1,512,1024]{2,1,0:T(8,128)(2,1)}, u32[]{:S(2)}) copy-start(bf16[1,512,1024]{2,1,0:T(8,128)(2,1)} %param.8) | copy-start | bytes 3145732
  7.2 49.9 %all-gather.4.cloned.1.call-start = ((), (), s32[]{:S(2)}) async-start(), calls=%async_computation | async-start | bytes 2621440 | tf_op jit(solution)/shard_map/all_gather | solution.py:65
  7.9 95.2 %all-gather.8.cloned.1.call-start = ((), (), s32[]{:S(2)}) async-start(), calls=%async_computation.2 | async-start | bytes 2621440 | tf_op jit(solution)/shard_map/all_gather | solution.py:64
  8.7 140.5 %all-gather.6.cloned.1.call-start = ((), (), s32[]{:S(2)}) async-start(), calls=%async_computation.1 | async-start | bytes 2621440 | tf_op jit(solution)/shard_map/all_gather | solution.py:63
  61.4 96.5 %collective-permute-start.1 = (bf16[1,32,1024]{2,1,0:T(8,128)(2,1)}, bf16[1,32,1024]{2,1,0:T(8,128)(2,1)S(1)}, u32[]{:S(2)}, u32[]{:S(2)}) collective-permute-start(bf16[1,32,1024]{2,1,0:T(8,128)(2,1)} %get-tuple-element.268), channel_id=1, source_target_pairs={{1,0},{2,1},{3,2},{4,3},{5,4},{6,5},{7,6},{9,8},{10,9},{11,10},{12... | collective-permute-start | bytes 196616 | tf_op jit(solution)/shard_map/ppermute | solution.py:14
  64.0 94.0 %collective-permute-start = (bf16[1,128,1024]{2,1,0:T(8,128)(2,1)}, bf16[1,128,1024]{2,1,0:T(8,128)(2,1)}, u32[]{:S(2)}, u32[]{:S(2)}) collective-permute-start(bf16[1,128,1024]{2,1,0:T(8,128)(2,1)} %slice.53), channel_id=1, source_target_pairs={{0,1},{1,2},{2,3},{3,4},{4,5},{5,6},{6,7},{8,9},{9,10},{10,11},{11... | collective-permute-start | bytes 786440 | tf_op jit(solution)/shard_map/ppermute | solution.py:14
  106.1 47.1 %copy-start.2 = (bf16[1,548,1024]{2,1,0:T(8,128)(2,1)}, bf16[1,548,1024]{2,1,0:T(8,128)(2,1)S(1)}, u32[]{:S(2)}) copy-start(bf16[1,548,1024]{2,1,0:T(8,128)(2,1)S(1)} %fusion.17) | copy-start | bytes 3366916
  106.9 54.0 %collective-permute-start.2 = (bf16[1,128,1024]{2,1,0:T(8,128)(2,1)}, bf16[1,128,1024]{2,1,0:T(8,128)(2,1)}, u32[]{:S(2)}, u32[]{:S(2)}) collective-permute-start(bf16[1,128,1024]{2,1,0:T(8,128)(2,1)} %slice.59), channel_id=1, source_target_pairs={{0,1},{1,2},{2,3},{3,4},{4,5},{5,6},{6,7},{8,9},{9,10},{10,11},{11... | collective-permute-start | bytes 786440 | tf_op jit(solution)/shard_map/ppermute | solution.py:14
  154.2 6.6 %slice-start = ((bf16[1,548,1024]{2,1,0:T(8,128)(2,1)}), bf16[1,512,1024]{2,1,0:T(8,128)(2,1)S(1)}, s32[]{:S(2)}) async-start(bf16[1,548,1024]{2,1,0:T(8,128)(2,1)} %copy-done.2), calls=%async_computation.3 | async-start | bytes 2097152 | tf_op jit(solution)/shard_map/slice | solution.py:73
  154.2 6.6 %collective-permute-start.3 = (bf16[1,32,1024]{2,1,0:T(8,128)(2,1)S(1)}, bf16[1,32,1024]{2,1,0:T(8,128)(2,1)S(1)}, u32[]{:S(2)}, u32[]{:S(2)}) collective-permute-start(bf16[1,32,1024]{2,1,0:T(8,128)(2,1)S(1)} %get-tuple-element.266), channel_id=1, source_target_pairs={{1,0},{2,1},{3,2},{4,3},{5,4},{6,5},{7,6},{9,8},{10,9},{11,10},{12... | collective-permute-start | bytes 196616 | tf_op jit(solution)/shard_map/ppermute | solution.py:14
  163.1 1.8 copy-start
  179.6 1.7 copy-start.1
  181.3 1.8 copy-start
  197.8 1.7 copy-start.1
  199.5 1.8 copy-start
  216.0 1.7 copy-start.1
  217.7 1.8 copy-start
  234.2 1.7 copy-start.1
Sparse Core Ops, SparseCore 0:
  9.5 47.5 all-gather.3
  58.7 44.4 all-gather.7
  104.7 44.4 all-gather.5
where the time goes:
time: 254 us; the launch traced here: 253 us
  waiting for transfers between devices  112 us (44%)
  local copies, waits for them, and re-layouts  37.7 us (15%)
  matrix products  33.9 us (13%)
  other arithmetic  18.3 us (7%)
  between operations  14.5 us (6%)
  loops' own time  13.5 us (5%)
  starting transfers between devices  12.8 us (5%)
  blocking collectives  9.73 us (4%)
    all_gather x1, waiting for transfers between devices, local(): q_flat = project_one(lax.all_gather(w_query, 'dp', axis=1, tiled=True))  38.7 us
    all_gather x1, waiting for transfers between devices, local(): k_flat = project_one(lax.all_gather(w_key, 'dp', axis=1, tiled=True))  35.3 us
    all_gather x1, waiting for transfers between devices, local(): v_flat = project_one(lax.all_gather(w_value, 'dp', axis=1, tiled=True))  34.8 us
    another operation x1, loops' own time, local(): attended = lax.map(one_segment, jnp.arange(seg_dev, dtype=jnp.int32))  13.5 us
    ppermute x4, starting transfers between devices, passed_along(): return lax.ppermute(block, axis, route)  12.7 us
    sub x4, matrix products, attend(): probs = jnp.exp(scores - row_max)  12.1 us
    dot_general x4, matrix products, attend(): jnp.einsum('bhqk,bkhe->bqhe', weights, v_heads, preferred_element_type=jn...  11.6 us
    all_gather x1, blocking collectives, local(): bank_rows = lax.all_gather(memory_in, 'seq', axis=1, tiled=True)  9.73 us
  transfers between devices with their start and end apart: 7, of which 4 were waited for; matrix products, arithmetic and copies ran while one was open for 7% of the time, Pallas kernels for 0%

commit v1 on v0

--- a/solution.py
+++ b/solution.py
@@ -6,6 +6,11 @@
 HEADS = 16
 LEFT = 128
 RIGHT = 32
+
+
+def gather_by_exchange(x, axis, dim):
+    copies = jnp.concatenate([x] * lax.axis_size(axis), axis=dim)
+    return lax.all_to_all(copies, axis, dim, dim, tiled=True)
 
 
 def passed_along(block, axis, distance):
@@ -60,7 +65,7 @@
     def project_one(piece):
         return jnp.dot(flat_rows, piece, preferred_element_type=jnp.float32).astype(jnp.bfloat16)
 
-    q_flat = project_one(lax.all_gather(w_query, "dp", axis=1, tiled=True))
+    q_flat = project_one(gather_by_exchange(w_query, "dp", 1))
     k_flat = project_one(lax.all_gather(w_key, "dp", axis=1, tiled=True))
     v_flat = project_one(lax.all_gather(w_value, "dp", axis=1, tiled=True))
     q_all = q_flat.reshape(utt_count, n_total, feat_width)

time: 254 us -> 264 us (1.039)
  local copies, waits for them, and re-layouts: 37.7 us -> 45 us
  starting transfers between devices: 12.8 us -> 16.9 us
  waiting for transfers between devices: 112 us -> 109 us
    all_gather x1 -> x0, waiting for transfers between devices: 38.7 us -> none  [local(): q_flat = project_one(lax.all_gather(w_query, 'dp', axis=1, tiled=True))]
    all_gather x1, waiting for transfers between devices: 34.8 us -> 66.2 us  [local(): v_flat = project_one(lax.all_gather(w_value, 'dp', axis=1, tiled=True))]
    all_to_all x0 -> x2, local copies, waits for them, and re-layouts: none -> 5.17 us  [gather_by_exchange(): return lax.all_to_all(copies, axis, dim, dim, tiled=True)]
    all_to_all x0 -> x1, starting transfers between devices: none -> 4.72 us  [gather_by_exchange(): return lax.all_to_all(copies, axis, dim, dim, tiled=True)]
    all_gather x1, waiting for transfers between devices: 35.3 us -> 39.6 us  [local(): k_flat = project_one(lax.all_gather(w_key, 'dp', axis=1, tiled=True))]
  transfers between devices with their start and end apart: 7 -> 7, of which waited for: 4 -> 3; matrix products, arithmetic and copies ran while one was open for 7% -> 9% of each run, Pallas kernels for 0% -> 0%
where the time goes in v1:
time: 264 us; the launch traced here: 262 us
  waiting for transfers between devices  109 us (41%)
  local copies, waits for them, and re-layouts  45 us (17%)
  matrix products  33.5 us (13%)
  other arithmetic  19.1 us (7%)
  starting transfers between devices  16.9 us (6%)
  between operations  14.9 us (6%)
  loops' own time  13.4 us (5%)
  blocking collectives  10 us (4%)
    all_gather x1, waiting for transfers between devices, local(): v_flat = project_one(lax.all_gather(w_value, 'dp', axis=1, tiled=True))  66.2 us
    all_gather x1, waiting for transfers between devices, local(): k_flat = project_one(lax.all_gather(w_key, 'dp', axis=1, tiled=True))  39.6 us
    another operation x1, loops' own time, local(): attended = lax.map(one_segment, jnp.arange(seg_dev, dtype=jnp.int32))  13.4 us
    ppermute x4, starting transfers between devices, passed_along(): return lax.ppermute(block, axis, route)  12.1 us
    sub x4, matrix products, attend(): probs = jnp.exp(scores - row_max)  12 us
    dot_general x4, matrix products, attend(): jnp.einsum('bhqk,bkhe->bqhe', weights, v_heads, preferred_element_type=jn...  11.6 us
    all_gather x1, blocking collectives, local(): bank_rows = lax.all_gather(memory_in, 'seq', axis=1, tiled=True)  10 us
    dot_general x3, matrix products, project_one(): jnp.dot(flat_rows, piece, preferred_element_type=jnp.float32)  9.65 us
  transfers between devices with their start and end apart: 7, of which 3 were waited for; matrix products, arithmetic and copies ran while one was open for 9% of the time, Pallas kernels for 0%

profile of v1, /device:TPU:3, one launch (start us, length us, event | category | flops | bytes accessed | tf_op | source)
XLA Modules:
  0.0 262.3 jit_solution(12377242104426659337)
XLA Ops:
  8.6 1.2 copy.44
  10.2 2.6 %copy.48 = bf16[1024,4,256]{2,0,1:T(8,128)(2,1)} copy(bf16[1024,4,256]{0,2,1:T(8,128)(2,1)S(1)} %bitcast.79) | data formatting | bytes 4194304 | tf_op jit(solution)/shard_map/all_to_all | solution.py:13
  12.8 4.7 %all-to-all-start = ((bf16[1024,4,256]{2,0,1:T(8,128)(2,1)}), bf16[1024,4,256]{2,0,1:T(8,128)(2,1)S(1)}, u32[]{:S(2)}, u32[]{:S(2)}) async-start(bf16[1024,4,256]{2,0,1:T(8,128)(2,1)} %copy.48), calls=%async_computation | async-start | bytes 4194304 | tf_op jit(solution)/shard_map/all_to_all | solution.py:13
  18.2 10.0 %all_gather.9 = bf16[1,32,1024]{2,0,1:T(2,128)(2,1)S(1)} all-gather(bf16[1,4,1024]{2,0,1:T(2,128)(2,1)S(1)} %copy.42), channel_id=1, replica_groups=mesh['dp'=4,'seq'=8] {'seq'}, dimensions={1}, use_global_device_ids=true | all-gather | bytes 73728 | tf_op jit(solution)/shard_map/all_gather | solution.py:48
  29.3 66.2 %all-gather.3.cloned.1.call-done = bf16[1024,1024]{1,0:T(8,128)(2,1)} async-done(((bf16[1024,256]{1,0:T(8,128)(2,1)}), bf16[1024,1024]{1,0:T(8,128)(2,1)}) %all-gather.3.cloned.1.call-update) | async-done | bytes 2097168 | tf_op jit(solution)/shard_map/all_gather | solution.py:70
  95.5 2.9 %fusion.15 = bf16[1,548,1024]{2,1,0:T(8,128)(2,1)S(1)} fusion(bf16[1024,1024]{1,0:T(8,128)(2,1)} %all-gather.3.cloned.1.call-done, bf16[1,32,1024]{2,1,0:T(8,128)(2,1)S(1)} %copy.43, bf16[1,4,1024]{2,1,0:T(4,128)(2,1)S(1)} %fusion.20, bf16[1,512,1024]{2,1,0:T(8,128)(2,1)S(1)} %copy-done.5), kind=kOutput, calls=%fused_computation.31 | convolution fusion | flops 1153167360 | bytes 4341760 | tf_op jit(solution)/shard_map/dot_general | solution.py:66
  98.5 1.0 copy-done.3
  100.2 2.4 collective-permute-start.1
  102.6 4.1 %collective-permute-start = (bf16[1,128,1024]{2,1,0:T(8,128)(2,1)S(1)}, bf16[1,128,1024]{2,1,0:T(8,128)(2,1)}, u32[]{:S(2)}, u32[]{:S(2)}) collective-permute-start(bf16[1,128,1024]{2,1,0:T(8,128)(2,1)S(1)} %slice.53), channel_id=1, source_target_pairs={{0,1},{1,2},{2,3},{3,4},{4,5},{5,6},{6,7},{8,9},{9,10},{10,11},{11... | collective-permute-start | bytes 786440 | tf_op jit(solution)/shard_map/ppermute | solution.py:19
  106.6 39.6 %all-gather.5.cloned.1.call-done = bf16[1024,1024]{1,0:T(8,128)(2,1)} async-done(((bf16[1024,256]{1,0:T(8,128)(2,1)}), bf16[1024,1024]{1,0:T(8,128)(2,1)}) %all-gather.5.cloned.1.call-update) | async-done | bytes 2097168 | tf_op jit(solution)/shard_map/all_gather | solution.py:69
  146.3 3.3 %fusion.17 = bf16[1,548,1024]{2,1,0:T(8,128)(2,1)S(1)} fusion(bf16[1024,1024]{1,0:T(8,128)(2,1)} %all-gather.5.cloned.1.call-done, bf16[1,32,1024]{2,1,0:T(8,128)(2,1)} %copy-done.7, bf16[1,4,1024]{2,1,0:T(4,128)(2,1)} %copy-done.9, bf16[1,512,1024]{2,1,0:T(8,128)(2,1)} %param.8), kind=kOutput, calls=%fused_computation.33 | convolution fusion | flops 1153167360 | bytes 4341760 | tf_op jit(solution)/shard_map/dot_general | solution.py:66
  150.3 3.6 %collective-permute-start.2 = (bf16[1,128,1024]{2,1,0:T(8,128)(2,1)}, bf16[1,128,1024]{2,1,0:T(8,128)(2,1)}, u32[]{:S(2)}, u32[]{:S(2)}) collective-permute-start(bf16[1,128,1024]{2,1,0:T(8,128)(2,1)} %slice.59), channel_id=1, source_target_pairs={{0,1},{1,2},{2,3},{3,4},{4,5},{5,6},{6,7},{8,9},{9,10},{10,11},{11... | collective-permute-start | bytes 786440 | tf_op jit(solution)/shard_map/ppermute | solution.py:19
  154.0 2.5 copy.49
  156.5 3.4 %fusion.16 = bf16[1,548,1024]{2,1,0:T(8,128)(2,1)S(1)} fusion(bf16[1024,1024]{0,1:T(8,128)(2,1)} %bitcast.80, bf16[1,32,1024]{2,1,0:T(8,128)(2,1)} %copy-done.7, bf16[1,4,1024]{2,1,0:T(4,128)(2,1)} %copy-done.9, bf16[1,512,1024]{2,1,0:T(8,128)(2,1)} %param.8), kind=kOutput, calls=%fused_computation.32 | convolution fusion | flops 1153167360 | bytes 4341760 | tf_op jit(solution)/shard_map/dot_general | solution.py:66
  160.5 1.0 slice.54
  161.6 1.0 slice.57
  163.2 2.1 collective-permute-start.3
  166.4 1.4 pad_maximum_fusion.4
  167.8 2.1 collective-permute-done.3
  169.9 2.2 pad_maximum_fusion.5
  172.1 72.8 %while.13 = (s32[]{:T(128)}, f32[4,1,129,1024]{2,3,1,0:T(8,128)}, s32[4]{0:T(128)S(1)}, bf16[1,672,1024]{2,1,0:T(8,128)(2,1)S(1)}, bf16[1,32,1024]{1,2,0:T(8,128...) while((s32[]{:T(128)}, f32[4,1,129,1024]{2,3,1,0:T(8,128)}, ...), condition=%wide.region_4.5_spmd.clone, body=%wide.region_1.4_spmd.clone.sunk | while | flops 176197520 | bytes 28918032 | solution.py:106
  173.9 1.1 constant_dynamic-slice_fusion.9
  175.4 1.8 pad_maximum_fusion.8
  182.7 3.0 %fusion.45 = (f32[16,129]{1,0:T(8,128)S(1)}, f32[16,129,320]{2,1,0:T(8,128)}) fusion(pred[320]{0:T(512)(128)(4,1)S(1)} %add_reduce_fusion.2, bf16[129,16,64]{0,2,1:T(8,128)(2,1)S(1)} %bitcast.78, bf16[320,16,64]{0,2,1:T(8,128)(2,1)S(1)} %bitcast.77), kind=kOutput, calls=%fused_computation.51.clone.1 | convolution fusion | flops 87183680 | bytes 3570048 | tf_op jit(solution)/shard_map/while/body/eval_jaxpr/sub | solution.py:33
  185.7 2.9 %fusion.46 = f32[16,64,129]{2,1,0:T(8,128)S(1)} fusion(bf16[320,16,64]{0,2,1:T(8,128)(2,1)S(1)} %bitcast.76, f32[16,129,320]{2,1,0:T(8,128)} %get-tuple-element.367, f32[16,129]{1,0:T(8,128)S(1)} %get-tuple-element.368), kind=kOutput, calls=%fused_computation.9.clone.1 | convolution fusion | flops 85862400 | bytes 3833920 | tf_op jit(solution)/shard_map/while/body/eval_jaxpr/bhqk,bkhe->bqhe/dot_general | solution.py:35
  188.6 1.1 constant_dynamic-update-slice_fusion.2
  192.1 1.1 constant_dynamic-slice_fusion.9
  193.6 1.8 pad_maximum_fusion.8
  195.4 1.0 constant_dynamic-slice_fusion.11
  200.9 3.0 %fusion.45 = (f32[16,129]{1,0:T(8,128)S(1)}, f32[16,129,320]{2,1,0:T(8,128)}) fusion(pred[320]{0:T(512)(128)(4,1)S(1)} %add_reduce_fusion.2, bf16[129,16,64]{0,2,1:T(8,128)(2,1)S(1)} %bitcast.78, bf16[320,16,64]{0,2,1:T(8,128)(2,1)S(1)} %bitcast.77), kind=kOutput, calls=%fused_computation.51.clone.1 | convolution fusion | flops 87183680 | bytes 3570048 | tf_op jit(solution)/shard_map/while/body/eval_jaxpr/sub | solution.py:33
  203.9 2.9 %fusion.46 = f32[16,64,129]{2,1,0:T(8,128)S(1)} fusion(bf16[320,16,64]{0,2,1:T(8,128)(2,1)S(1)} %bitcast.76, f32[16,129,320]{2,1,0:T(8,128)} %get-tuple-element.367, f32[16,129]{1,0:T(8,128)S(1)} %get-tuple-element.368), kind=kOutput, calls=%fused_computation.9.clone.1 | convolution fusion | flops 85862400 | bytes 3833920 | tf_op jit(solution)/shard_map/while/body/eval_jaxpr/bhqk,bkhe->bqhe/dot_general | solution.py:35
  206.8 1.1 constant_dynamic-update-slice_fusion.2
  210.3 1.1 constant_dynamic-slice_fusion.9
  211.8 1.8 pad_maximum_fusion.8
  213.6 1.0 constant_dynamic-slice_fusion.11
  219.1 3.0 %fusion.45 = (f32[16,129]{1,0:T(8,128)S(1)}, f32[16,129,320]{2,1,0:T(8,128)}) fusion(pred[320]{0:T(512)(128)(4,1)S(1)} %add_reduce_fusion.2, bf16[129,16,64]{0,2,1:T(8,128)(2,1)S(1)} %bitcast.78, bf16[320,16,64]{0,2,1:T(8,128)(2,1)S(1)} %bitcast.77), kind=kOutput, calls=%fused_computation.51.clone.1 | convolution fusion | flops 87183680 | bytes 3570048 | tf_op jit(solution)/shard_map/while/body/eval_jaxpr/sub | solution.py:33
  222.1 2.9 %fusion.46 = f32[16,64,129]{2,1,0:T(8,128)S(1)} fusion(bf16[320,16,64]{0,2,1:T(8,128)(2,1)S(1)} %bitcast.76, f32[16,129,320]{2,1,0:T(8,128)} %get-tuple-element.367, f32[16,129]{1,0:T(8,128)S(1)} %get-tuple-element.368), kind=kOutput, calls=%fused_computation.9.clone.1 | convolution fusion | flops 85862400 | bytes 3833920 | tf_op jit(solution)/shard_map/while/body/eval_jaxpr/bhqk,bkhe->bqhe/dot_general | solution.py:35
  225.0 1.0 constant_dynamic-update-slice_fusion.2
  228.5 1.1 constant_dynamic-slice_fusion.9
  230.0 1.8 pad_maximum_fusion.8
  231.8 1.0 constant_dynamic-slice_fusion.11
  237.3 3.0 %fusion.45 = (f32[16,129]{1,0:T(8,128)S(1)}, f32[16,129,320]{2,1,0:T(8,128)}) fusion(pred[320]{0:T(512)(128)(4,1)S(1)} %add_reduce_fusion.2, bf16[129,16,64]{0,2,1:T(8,128)(2,1)S(1)} %bitcast.78, bf16[320,16,64]{0,2,1:T(8,128)(2,1)S(1)} %bitcast.77), kind=kOutput, calls=%fused_computation.51.clone.1 | convolution fusion | flops 87183680 | bytes 3570048 | tf_op jit(solution)/shard_map/while/body/eval_jaxpr/sub | solution.py:33
  240.3 2.9 %fusion.46 = f32[16,64,129]{2,1,0:T(8,128)S(1)} fusion(bf16[320,16,64]{0,2,1:T(8,128)(2,1)S(1)} %bitcast.76, f32[16,129,320]{2,1,0:T(8,128)} %get-tuple-element.367, f32[16,129]{1,0:T(8,128)S(1)} %get-tuple-element.368), kind=kOutput, calls=%fused_computation.9.clone.1 | convolution fusion | flops 85862400 | bytes 3833920 | tf_op jit(solution)/shard_map/while/body/eval_jaxpr/bhqk,bkhe->bqhe/dot_general | solution.py:35
  243.2 1.1 constant_dynamic-update-slice_fusion.2
  244.9 3.1 %slice.51 = f32[4,1,128,1024]{2,3,1,0:T(8,128)} slice(f32[4,1,129,1024]{2,3,1,0:T(8,128)} %get-tuple-element.165), slice={[0:4], [0:1], [0:128], [0:1024]} | slice | bytes 4194304 | tf_op jit(solution)/shard_map/slice | solution.py:108
  248.0 3.7 %copy.57 = bf16[4,1,129,1024]{3,0,2,1:T(4,128)(2,1)S(1)} copy(f32[4,1,129,1024]{2,3,1,0:T(8,128)} %get-tuple-element.165) | data formatting | bytes 3170304 | tf_op jit(solution)/shard_map/while | solution.py:106
  251.7 1.9 copy.56
  254.3 1.1 fusion.14
  (107 shorter events, 23.9 us)
Async XLA Ops:
  7.2 88.4 %all-gather.3.cloned.1.call-start = ((), (), s32[]{:S(2)}) async-start(), calls=%async_computation.1 | async-start | bytes 2621440 | tf_op jit(solution)/shard_map/all_gather | solution.py:70
  7.9 138.4 %all-gather.5.cloned.1.call-start = ((), (), s32[]{:S(2)}) async-start(), calls=%async_computation.2 | async-start | bytes 2621440 | tf_op jit(solution)/shard_map/all_gather | solution.py:69
  12.8 5.4 %copy-start.8 = (bf16[1,4,1024]{2,1,0:T(4,128)(2,1)S(1)}, bf16[1,4,1024]{2,1,0:T(4,128)(2,1)}, u32[]{:S(2)}) copy-start(bf16[1,4,1024]{2,1,0:T(4,128)(2,1)} %param.9) | copy-start | bytes 24580
  12.8 16.2 %copy-start.5 = (bf16[1,512,1024]{2,1,0:T(8,128)(2,1)S(1)}, bf16[1,512,1024]{2,1,0:T(8,128)(2,1)}, u32[]{:S(2)}) copy-start(bf16[1,512,1024]{2,1,0:T(8,128)(2,1)} %param.8) | copy-start | bytes 3145732
  12.8 141.1 %all-to-all-start = ((bf16[1024,4,256]{2,0,1:T(8,128)(2,1)}), bf16[1024,4,256]{2,0,1:T(8,128)(2,1)S(1)}, u32[]{:S(2)}, u32[]{:S(2)}) async-start(bf16[1024,4,256]{2,0,1:T(8,128)(2,1)} %copy.48), calls=%async_computation | async-start | bytes 4194304 | tf_op jit(solution)/shard_map/all_to_all | solution.py:13
  28.3 70.2 %copy-start.7 = (bf16[1,32,1024]{2,1,0:T(8,128)(2,1)}, bf16[1,32,1024]{2,1,0:T(8,128)(2,1)S(1)}, u32[]{:S(2)}) copy-start(bf16[1,32,1024]{2,1,0:T(8,128)(2,1)S(1)} %copy.43) | copy-start | bytes 196612
  29.3 69.2 %copy-start.9 = (bf16[1,4,1024]{2,1,0:T(4,128)(2,1)}, bf16[1,4,1024]{2,1,0:T(4,128)(2,1)S(1)}, u32[]{:S(2)}) copy-start(bf16[1,4,1024]{2,1,0:T(4,128)(2,1)S(1)} %fusion.20) | copy-start | bytes 24580
  98.5 1.1 copy-start.3
  100.2 66.2 %collective-permute-start.1 = (bf16[1,32,1024]{2,1,0:T(8,128)(2,1)}, bf16[1,32,1024]{2,1,0:T(8,128)(2,1)}, u32[]{:S(2)}, u32[]{:S(2)}) collective-permute-start(bf16[1,32,1024]{2,1,0:T(8,128)(2,1)} %get-tuple-element.281), channel_id=1, source_target_pairs={{1,0},{2,1},{3,2},{4,3},{5,4},{6,5},{7,6},{9,8},{10,9},{11,10},{12... | collective-permute-start | bytes 196616 | tf_op jit(solution)/shard_map/ppermute | solution.py:19
  102.6 63.8 %collective-permute-start = (bf16[1,128,1024]{2,1,0:T(8,128)(2,1)S(1)}, bf16[1,128,1024]{2,1,0:T(8,128)(2,1)}, u32[]{:S(2)}, u32[]{:S(2)}) collective-permute-start(bf16[1,128,1024]{2,1,0:T(8,128)(2,1)S(1)} %slice.53), channel_id=1, source_target_pairs={{0,1},{1,2},{2,3},{3,4},{4,5},{5,6},{6,7},{8,9},{9,10},{10,11},{11... | collective-permute-start | bytes 786440 | tf_op jit(solution)/shard_map/ppermute | solution.py:19
  149.6 12.0 %copy-start.2 = (bf16[1,548,1024]{2,1,0:T(8,128)(2,1)}, bf16[1,548,1024]{2,1,0:T(8,128)(2,1)S(1)}, u32[]{:S(2)}) copy-start(bf16[1,548,1024]{2,1,0:T(8,128)(2,1)S(1)} %fusion.17) | copy-start | bytes 3366916
  150.3 19.6 %collective-permute-start.2 = (bf16[1,128,1024]{2,1,0:T(8,128)(2,1)}, bf16[1,128,1024]{2,1,0:T(8,128)(2,1)}, u32[]{:S(2)}, u32[]{:S(2)}) collective-permute-start(bf16[1,128,1024]{2,1,0:T(8,128)(2,1)} %slice.59), channel_id=1, source_target_pairs={{0,1},{1,2},{2,3},{3,4},{4,5},{5,6},{6,7},{8,9},{9,10},{10,11},{11... | collective-permute-start | bytes 786440 | tf_op jit(solution)/shard_map/ppermute | solution.py:19
  156.5 4.1 %copy-start.4 = (bf16[1,548,1024]{2,1,0:T(8,128)(2,1)S(1)}, bf16[1,548,1024]{2,1,0:T(8,128)(2,1)}, u32[]{:S(2)}) copy-start(bf16[1,548,1024]{2,1,0:T(8,128)(2,1)} %copy-done.3) | copy-start | bytes 3366916
  162.6 7.3 %slice-start = ((bf16[1,548,1024]{2,1,0:T(8,128)(2,1)}), bf16[1,512,1024]{2,1,0:T(8,128)(2,1)S(1)}, s32[]{:S(2)}) async-start(bf16[1,548,1024]{2,1,0:T(8,128)(2,1)} %copy-done.2), calls=%async_computation.3 | async-start | bytes 2097152 | tf_op jit(solution)/shard_map/slice | solution.py:78
  163.2 6.7 %collective-permute-start.3 = (bf16[1,32,1024]{2,1,0:T(8,128)(2,1)}, bf16[1,32,1024]{2,1,0:T(8,128)(2,1)S(1)}, u32[]{:S(2)}, u32[]{:S(2)}) collective-permute-start(bf16[1,32,1024]{2,1,0:T(8,128)(2,1)} %get-tuple-element.279), channel_id=1, source_target_pairs={{1,0},{2,1},{3,2},{4,3},{5,4},{6,5},{7,6},{9,8},{10,9},{11,10},{12... | collective-permute-start | bytes 196616 | tf_op jit(solution)/shard_map/ppermute | solution.py:19
  166.4 5.8 %copy-start.6 = (bf16[1,4,1024]{2,1,0:T(4,128)(2,1)S(1)}, bf16[1,4,1024]{2,1,0:T(4,128)(2,1)}, u32[]{:S(2)}) copy-start(bf16[1,4,1024]{2,1,0:T(4,128)(2,1)} %slice.58) | copy-start | bytes 24580
  172.1 1.8 copy-start
  188.6 1.7 copy-start.1
  190.3 1.8 copy-start
  206.8 1.7 copy-start.1
  208.5 1.8 copy-start
  225.0 1.7 copy-start.1
  226.7 1.8 copy-start
  243.2 1.7 copy-start.1
  251.7 2.5 copy-start.10
Sparse Core Ops, SparseCore 0:
  9.5 85.9 all-gather.2
  97.1 49.1 all-gather.4
